TPU v7x, 256 devices: a whole 4x4x8 slice. The times are simulated.
256 devices in a mesh: seq: 64 (over y, z, core), section: 4 (over x).
Axes of the slice: x: 4, y: 4, z: 8, core: 2. Of those that a mesh axis runs over, the one named last changes fastest.
Arguments:
- acts: bfloat16 [16384, 1408], P('seq'), may hold values from -16 to 16
- pre_act: bfloat16 [16384, 1536], P('seq', 'section'), may hold values from -6 to 6
- emb_grad: bfloat16 [8192, 1536], P('seq', 'section'), may hold values from -6 to 6
- filters: bfloat16 [7040, 1536], P('seq', 'section'), may hold values from -0.0625 to 0.0625
Outputs:
- input_grad: bfloat16 [16384, 1408], P('seq', 'section')
- filter_grad: float32 [7040, 1536], P('seq', 'section')
All inputs are finite; a program needn't handle non-finite values.
Results may differ from a plain program's by a relative error of at most 0.0049.
Values may be sent and summed in bfloat16 or wider, within the bound.
A program may use at most 128 MiB of HBM per device.

v0:
```python
import math
import jax
import jax.numpy as jnp
from jax import lax
from jax.sharding import PartitionSpec as P

KERNEL = 5
SEQS = 1


def with_halo(shard, sides, width):
    for axis, dim in sides:
        size, length = (lax.axis_size(axis), shard.shape[dim])
        up = [(i, (i + 1) % size) for i in range(size - 1)]
        down = [(j, i) for i, j in up]
        last = lax.slice_in_dim(shard, length - width, length, axis=dim)
        first = lax.slice_in_dim(shard, 0, width, axis=dim)
        before = lax.ppermute(last, axis, up)
        after = lax.ppermute(first, axis, down)
        shard = jnp.concatenate([before, shard, after], axis=dim)
    return shard


def gelu_slope(value):
    cumul = 0.5 * (1.0 + lax.erf(value * 0.7071067811865476))
    dens = jnp.exp(-0.5 * value * value) * 0.3989422804014327
    return cumul + value * dens


def shards(acts, pre_act, emb_grad, filters):
    rows = acts.shape[0]
    c_in = acts.shape[1]
    upward = jnp.repeat(emb_grad.astype(jnp.float32), 2, axis=0) * 0.5
    zvalue = pre_act.astype(jnp.float32)
    dz_grad = (upward * gelu_slope(zvalue)).astype(jnp.bfloat16)
    total_rows = rows * lax.axis_size("seq")
    length = total_rows // SEQS
    first = lax.axis_index("seq") * rows
    positions = first - 2 + jnp.arange(rows + 4, dtype=jnp.int32)
    inside = (jnp.floor_divide(positions, length) == first // length).astype(jnp.bfloat16)[:, None]
    scale_value = 1.0 / math.sqrt(total_rows)
    grad_rim = with_halo(dz_grad, (("seq", 0),), 2) * inside
    whole_term = (
        jnp.concatenate(
            [
                jnp.einsum(
                    "rc,ro->co",
                    acts,
                    grad_rim[4 - k : 4 - k + rows],
                    preferred_element_type=jnp.float32,
                )
                for k in range(KERNEL)
            ],
            axis=0,
        )
        * scale_value
    )
    piece = lax.all_gather(filters, "seq", axis=0, tiled=True)
    width = piece.shape[0]
    product = jnp.einsum("ro,no->rn", grad_rim, piece, preferred_element_type=jnp.float32)
    tap_of = jnp.arange(width, dtype=jnp.int32) // c_in
    total = jnp.zeros((rows, width), jnp.float32)
    for k in range(KERNEL):
        total = total + jnp.where((tap_of == k)[None, :], product[4 - k : 4 - k + rows], 0.0)
    partial_input = total.reshape(rows, KERNEL, c_in).sum(axis=1)
    input_grad = lax.psum_scatter(partial_input, "section", scatter_dimension=1, tiled=True).astype(
        jnp.bfloat16
    )
    filter_grad = lax.psum_scatter(whole_term, "seq", scatter_dimension=0, tiled=True)
    return (input_grad, filter_grad)


def solution(mesh):
    in_specs = (P("seq", None), P("seq", "section"), P("seq", "section"), P("seq", "section"))
    out_specs = (P("seq", "section"), P("seq", "section"))
    return jax.shard_map(shards, mesh=mesh, in_specs=in_specs, out_specs=out_specs, check_vma=False)
```

profile of v0, /device:TPU:8, one launch (start us, length us, event | category | flops | bytes accessed | tf_op | source)
XLA Modules:
  0.0 342.2 jit_solution(12863627836406627910)
XLA Ops:
  7.2 0.0 all-gather.3.cloned.1.call-start
  7.2 0.7 all-gather.3.cloned.1.call-update
  7.9 0.0 all-reduce.3.cloned.1.call-start
  8.0 0.9 convert_multiply_fusion.4
  8.9 0.1 broadcast_in_dim.46
  9.0 0.3 mul.55
  9.3 1.1 fusion.16
  10.4 7.1 %collective-permute-start.1 = (bf16[2,384]{1,0:T(2,128)(2,1)S(1)}, bf16[2,384]{1,0:T(2,128)(2,1)S(1)}, u32[]{:S(2)}, u32[]{:S(2)}) collective-permute-start(bf16[2,384]{1,0:T(2,128)(2,1)S(1)} %get-tuple-element.9), channel_id=1, source_target_pairs={{4,0},{8,4},{12,8},{16,12},{20,16},{24,20},{28,24},{32,28},{36,32}... | collective-permute-start | bytes 4616 | tf_op jit(solution)/shard_map/ppermute | solution.py:19
  17.5 1.9 collective-permute-start
  19.5 5.0 %collective-permute-done = bf16[2,384]{1,0:T(2,128)(2,1)S(1)} collective-permute-done((bf16[2,384]{1,0:T(2,128)(2,1)S(1)}, bf16[2,384]{1,0:T(2,128)(2,1)S(1)}, u32[]{:S(2)}, u32[]{:S(2)}) %collective-permute-start) | collective-permute-done | bytes 1568 | tf_op jit(solution)/shard_map/ppermute | solution.py:18
  24.5 0.1 maximum_multiply_fusion
  24.7 0.5 fusion.8
  25.2 0.5 fusion.7
  25.7 0.5 fusion.6
  26.2 0.5 fusion.5
  26.7 0.5 fusion.4
  27.2 4.6 %broadcast_multiply_fusion = f32[7040,384]{0,1:T(8,128)} fusion(f32[7040,384]{0,1:T(8,128)S(1)} %fusion.4), kind=kLoop, calls=%fused_computation.9 | loop fusion | flops 2703360 | bytes 21626880 | tf_op jit(solution)/shard_map/mul | solution.py:44
  31.8 0.0 all-reduce.3.cloned.1.call-update
  31.8 0.0 reduce-scatter.3.cloned.1.call-start
  32.0 60.9 %all-gather.3.cloned.1.call-done = bf16[64,110,384]{2,1,0:T(8,128)(2,1)} async-done(((bf16[1,110,384]{2,1,0:T(8,128)(2,1)}), bf16[64,110,384]{2,1,0:T(8,128)(2,1)}) %all-gather.3.cloned.1.call-update) | async-done | bytes 5406736 | tf_op jit(solution)/shard_map/all_gather | solution.py:58
  92.9 7.7 %reshape.59 = bf16[7040,384]{1,0:T(8,128)(2,1)} reshape(bf16[64,110,384]{2,1,0:T(8,128)(2,1)} %all-gather.3.cloned.1.call-done) | data formatting | bytes 10813440
  100.6 4.7 %fusion.30 = f32[260,7040]{1,0:T(8,128)S(1)} fusion(bf16[7040,384]{1,0:T(8,128)(2,1)} %reshape.59, bf16[2,384]{1,0:T(2,128)(2,1)S(1)} %collective-permute-done.1, bf16[256,384]{1,0:T(8,128)(2,1)S(1)} %fusion.16, bf16[2,384]{1,0:T(2,128)(2,1)S(1)} %collective-permute-done, bf16[260]{0:T(512)(128)(2,1)S(1)} %fusion.29), kind=kOutput, calls=%fused_computation.63 | convolution fusion | flops 1406545920 | bytes 12928520 | tf_op jit(solution)/shard_map/ro,no->rn/dot_general | solution.py:60
  105.3 6.0 %fusion = f32[256,7040]{1,0:T(8,128)} fusion(f32[260,7040]{1,0:T(8,128)S(1)} %fusion.30, pred[7040]{0:T(1024)(128)(4,1)S(1)} %get-tuple-element.10, pred[7040]{0:T(1024)(128)(4,1)S(1)} %get-tuple-element.11, pred[7040]{0:T(1024)(128)(4,1)S(1)} %get-tuple-element.12, pred[7040]{0:T(1024)(128)(4,1)S(1)} %broadcast_compare_fusion.4, ...), kind=kLoop, calls=%fused_computation.1 | loop fusion | flops 16220160 | bytes 43288960 | tf_op jit(solution)/shard_map/add | solution.py:64
  111.3 8.8 %copy.9 = f32[256,7040]{0,1:T(8,128)} copy(f32[256,7040]{1,0:T(8,128)} %fusion) | data formatting | bytes 14417920 | tf_op jit(solution)/shard_map/add | solution.py:64
  120.1 4.9 %reduce_sum.9 = f32[256,1408]{0,1:T(8,128)} reduce(f32[256,5,1408]{0,2,1:T(8,128)} %bitcast.31, f32[]{:T(128)} %constant.61.clone.1), dimensions={1}, to_apply=%region_0.1 | reduce | flops 1441792 | bytes 8650756 | tf_op jit(solution)/shard_map/reduce_sum | solution.py:65
  125.0 0.0 reduce-scatter.3.cloned.1.call-update
  125.1 0.6 dynamic-slice
  126.3 178.5 %all-reduce.3.cloned.1.call-done = f32[7040,384]{0,1:T(8,128)} async-done(((f32[7040,384]{0,1:T(8,128)}), f32[7040,384]{0,1:T(8,128)}) %all-reduce.3.cloned.1.call-update) | async-done | bytes 10813456
  304.9 1.1 constant_dynamic-slice_fusion
  306.0 0.8 copy.10
  306.8 27.2 %reduce-scatter.3.cloned.1.call-done = f32[256,352]{0,1:T(8,128)} async-done(((f32[256,1408]{0,1:T(8,128)}), f32[256,352]{0,1:T(8,128)}) %reduce-scatter.3.cloned.1.call-update) | async-done | bytes 360464 | tf_op jit(solution)/shard_map/reduce_scatter | solution.py:66
  334.0 1.7 convert_element_type.23
  (12 shorter events, 0.1 us)
Async XLA Ops:
  7.2 17.5 %copy-start = (bf16[256,1408]{1,0:T(8,128)(2,1)S(1)}, bf16[256,1408]{1,0:T(8,128)(2,1)}, u32[]{:S(2)}) copy-start(bf16[256,1408]{1,0:T(8,128)(2,1)} %param.4) | copy-start | bytes 2162692
  7.2 85.7 %all-gather.3.cloned.1.call-start = ((), (), s32[]{:S(2)}) async-start(), calls=%async_computation.2 | async-start | bytes 5591040 | tf_op jit(solution)/shard_map/all_gather | solution.py:58
  7.9 297.0 %all-reduce.3.cloned.1.call-start = ((), (), s32[]{:S(2)}) async-start(), calls=%async_computation.3 | async-start | bytes 21626880
  10.4 9.1 %collective-permute-start.1 = (bf16[2,384]{1,0:T(2,128)(2,1)S(1)}, bf16[2,384]{1,0:T(2,128)(2,1)S(1)}, u32[]{:S(2)}, u32[]{:S(2)}) collective-permute-start(bf16[2,384]{1,0:T(2,128)(2,1)S(1)} %get-tuple-element.9), channel_id=1, source_target_pairs={{4,0},{8,4},{12,8},{16,12},{20,16},{24,20},{28,24},{32,28},{36,32}... | collective-permute-start | bytes 4616 | tf_op jit(solution)/shard_map/ppermute | solution.py:19
  17.5 7.0 %collective-permute-start = (bf16[2,384]{1,0:T(2,128)(2,1)S(1)}, bf16[2,384]{1,0:T(2,128)(2,1)S(1)}, u32[]{:S(2)}, u32[]{:S(2)}) collective-permute-start(bf16[2,384]{1,0:T(2,128)(2,1)S(1)} %get-tuple-element.8), channel_id=1, source_target_pairs={{0,4},{4,8},{8,12},{12,16},{16,20},{20,24},{24,28},{28,32},{32,36}... | collective-permute-start | bytes 4616 | tf_op jit(solution)/shard_map/ppermute | solution.py:18
  31.8 302.2 %reduce-scatter.3.cloned.1.call-start = ((), (), s32[]{:S(2)}) async-start(), calls=%async_computation.1 | async-start | bytes 1802240 | tf_op jit(solution)/shard_map/reduce_scatter | solution.py:66
  111.3 224.4 %copy-start.1 = (bf16[256,1408]{1,0:T(8,128)(2,1)S(1)}, bf16[256,1408]{1,0:T(8,128)(2,1)}, u32[]{:S(2)}) copy-start(bf16[256,1408]{1,0:T(8,128)(2,1)} %param.4) | copy-start | bytes 2162692
  120.1 5.0 %copy-start.2 = (u32[256]{0:T(256)S(1)}, u32[256]{0:T(256)}, u32[]{:S(2)}) copy-start(u32[256]{0:T(256)} %constant.69) | copy-start | bytes 3076
Sparse Core Ops, SparseCore 0:
  10.7 82.1 all-gather.2
  96.5 208.2 all-reduce.2
  307.6 26.3 reduce-scatter.2
where the time goes:
time: 343 us; the launch traced here: 342 us
  waiting for transfers between devices  272 us (79%)
  local copies, waits for them, and re-layouts  19.5 us (6%)
  other arithmetic  19.4 us (6%)
  between operations  14.6 us (4%)
  starting transfers between devices  9.13 us (3%)
  matrix products  7.19 us (2%)
    unnamed x4, waiting for transfers between devices  179 us
    all_gather x1, waiting for transfers between devices, shards(): piece = lax.all_gather(filters, 'seq', axis=0, tiled=True)  60.9 us
    reduce_scatter x1, waiting for transfers between devices, shards(): lax.psum_scatter(partial_input, 'section', scatter_dimension=1, tiled=True)  27.2 us
    unnamed x10, local copies, waits for them, and re-layouts  10.3 us
    add x1, local copies, waits for them, and re-layouts, shards(): total + jnp.where((tap_of == k)[None, :], product[4 - k:4 - k + rows], 0.0)  8.77 us
    ppermute x1, starting transfers between devices, with_halo(): after = lax.ppermute(first, axis, down)  7.09 us
  transfers between devices with their start and end apart: 5, of which 4 were waited for; matrix products, arithmetic and copies ran while one was open for 13% of the time, Pallas kernels for 0%

commit v1 on v0

--- a/solution.py
+++ b/solution.py
@@ -55,7 +55,9 @@
         )
         * scale_value
     )
-    piece = lax.all_gather(filters, "seq", axis=0, tiled=True)
+    piece = jnp.concatenate(
+        lax.all_to_all(jnp.stack([filters] * lax.axis_size("seq")), "seq", 0, 0), axis=0
+    )
     width = piece.shape[0]
     product = jnp.einsum("ro,no->rn", grad_rim, piece, preferred_element_type=jnp.float32)
     tap_of = jnp.arange(width, dtype=jnp.int32) // c_in

time: 343 us -> 374 us (1.090)
  waiting for transfers between devices: 272 us -> 290 us
  starting transfers between devices: 9.13 us -> 18.7 us
  local copies, waits for them, and re-layouts: 19.5 us -> 23.4 us
    ppermute x1, waiting for transfers between devices: 0.01 us -> 109 us  [with_halo(): after = lax.ppermute(first, axis, down)]
    all_gather x1 -> x0, waiting for transfers between devices: 60.9 us -> none  [shards(): piece = lax.all_gather(filters, 'seq', axis=0, tiled=True)]
    reduce_scatter x1, waiting for transfers between devices: 27.2 us -> 0.01 us  [shards(): lax.psum_scatter(partial_input, 'section', scatter_dimension=1, tiled=True)]
    all_to_all x0 -> x1, starting transfers between devices: none -> 12.4 us  [shards(): lax.all_to_all(jnp.stack([filters] * lax.axis_size('seq')), 'seq', 0, 0)]
    reshape x0 -> x1, local copies, waits for them, and re-layouts: none -> 7.77 us  [shards(): jnp.concatenate(lax.all_to_all(jnp.stack([filters] * lax.axis_size('seq')...]
    unnamed x10 -> x13, local copies, waits for them, and re-layouts: 10.3 us -> 2.53 us
    another operation x0 -> x1, local copies, waits for them, and re-layouts: none -> 3.9 us  [shards(): jnp.stack([filters] * lax.axis_size('seq'))]
    unnamed x4 -> x3, waiting for transfers between devices: 179 us -> 179 us
  transfers between devices with their start and end apart: 5 -> 5, of which waited for: 4 -> 3; matrix products, arithmetic and copies ran while one was open for 13% -> 11% of each run, Pallas kernels for 0% -> 0%
where the time goes in v1:
time: 374 us; the launch traced here: 373 us
  waiting for transfers between devices  290 us (78%)
  local copies, waits for them, and re-layouts  23.4 us (6%)
  starting transfers between devices  18.7 us (5%)
  other arithmetic  17.6 us (5%)
  between operations  16.3 us (4%)
  matrix products  7.19 us (2%)
    unnamed x3, waiting for transfers between devices  179 us
    ppermute x1, waiting for transfers between devices, with_halo(): after = lax.ppermute(first, axis, down)  109 us
    all_to_all x1, starting transfers between devices, shards(): lax.all_to_all(jnp.stack([filters] * lax.axis_size('seq')), 'seq', 0, 0)  12.4 us
    add x1, local copies, waits for them, and re-layouts, shards(): total + jnp.where((tap_of == k)[None, :], product[4 - k:4 - k + rows], 0.0)  8.76 us
    reshape x1, local copies, waits for them, and re-layouts, shards(): jnp.concatenate(lax.all_to_all(jnp.stack([filters] * lax.axis_size('seq')...  7.77 us
  transfers between devices with their start and end apart: 5, of which 3 were waited for; matrix products, arithmetic and copies ran while one was open for 11% of the time, Pallas kernels for 0%

profile of v1, /device:TPU:8, one launch (start us, length us, event | category | flops | bytes accessed | tf_op | source)
XLA Modules:
  0.0 373.3 jit_solution(4896163097983277382)
XLA Ops:
  8.0 0.0 copy-start
  8.0 3.9 %stack.2 = bf16[64,110,384]{2,1,0:T(8,128)(2,1)} broadcast(bf16[110,384]{1,0:T(8,128)(2,1)} %param.7), dimensions={1,2} | broadcast | bytes 5491200 | tf_op jit(solution)/shard_map/stack | solution.py:59
  11.9 12.4 %all-to-all-start = ((bf16[64,110,384]{2,1,0:T(8,128)(2,1)}), bf16[64,110,384]{2,1,0:T(8,128)(2,1)}, u32[]{:S(2)}, u32[]{:S(2)}) async-start(bf16[64,110,384]{2,1,0:T(8,128)(2,1)} %stack.2), calls=%async_computation | async-start | bytes 11010048 | tf_op jit(solution)/shard_map/all_to_all | solution.py:59
  24.3 0.0 all-reduce.3.cloned.1.call-start
  24.4 0.1 broadcast_in_dim.46
  24.6 0.3 mul.55
  24.9 0.2 fusion.16
  25.1 4.3 %collective-permute-start.1 = (bf16[2,384]{1,0:T(2,128)(2,1)S(1)}, bf16[2,384]{1,0:T(2,128)(2,1)S(1)}, u32[]{:S(2)}, u32[]{:S(2)}) collective-permute-start(bf16[2,384]{1,0:T(2,128)(2,1)S(1)} %get-tuple-element.9), channel_id=1, source_target_pairs={{4,0},{8,4},{12,8},{16,12},{20,16},{24,20},{28,24},{32,28},{36,32}... | collective-permute-start | bytes 4616 | tf_op jit(solution)/shard_map/ppermute | solution.py:19
  29.4 1.9 collective-permute-start
  31.4 109.3 %collective-permute-done.1 = bf16[2,384]{1,0:T(2,128)(2,1)S(1)} collective-permute-done((bf16[2,384]{1,0:T(2,128)(2,1)S(1)}, bf16[2,384]{1,0:T(2,128)(2,1)S(1)}, u32[]{:S(2)}, u32[]{:S(2)}) %collective-permute-start.1) | collective-permute-done | bytes 1568 | tf_op jit(solution)/shard_map/ppermute | solution.py:19
  140.7 2.0 collective-permute-done
  142.7 0.1 maximum_multiply_fusion
  142.8 0.5 fusion.8
  143.3 0.5 fusion.7
  143.8 0.5 fusion.6
  144.3 0.5 fusion.5
  144.8 0.5 fusion.4
  145.3 4.6 %broadcast_multiply_fusion = f32[7040,384]{0,1:T(8,128)} fusion(f32[7040,384]{0,1:T(8,128)S(1)} %fusion.4), kind=kLoop, calls=%fused_computation.9 | loop fusion | flops 2703360 | bytes 21626880 | tf_op jit(solution)/shard_map/mul | solution.py:44
  149.9 0.0 all-reduce.3.cloned.1.call-update
  150.0 0.0 reduce-scatter.3.cloned.1.call-start
  150.1 0.0 all-to-all-done
  150.1 7.8 %reshape.62 = bf16[7040,384]{1,0:T(8,128)(2,1)} reshape(bf16[64,110,384]{2,1,0:T(8,128)(2,1)} %all-to-all-done) | data formatting | bytes 10813440 | tf_op jit(solution)/shard_map/reshape | solution.py:58
  157.9 4.7 %fusion.30 = f32[260,7040]{1,0:T(8,128)S(1)} fusion(bf16[7040,384]{1,0:T(8,128)(2,1)} %reshape.62, bf16[2,384]{1,0:T(2,128)(2,1)S(1)} %collective-permute-done.1, bf16[256,384]{1,0:T(8,128)(2,1)S(1)} %fusion.16, bf16[2,384]{1,0:T(2,128)(2,1)S(1)} %collective-permute-done, bf16[260]{0:T(512)(128)(2,1)S(1)} %fusion.29), kind=kOutput, calls=%fused_computation.63 | convolution fusion | flops 1406545920 | bytes 12928520 | tf_op jit(solution)/shard_map/ro,no->rn/dot_general | solution.py:62
  162.6 6.0 %fusion = f32[256,7040]{1,0:T(8,128)} fusion(f32[260,7040]{1,0:T(8,128)S(1)} %fusion.30, pred[7040]{0:T(1024)(128)(4,1)S(1)} %get-tuple-element.10, pred[7040]{0:T(1024)(128)(4,1)S(1)} %get-tuple-element.11, pred[7040]{0:T(1024)(128)(4,1)S(1)} %get-tuple-element.12, pred[7040]{0:T(1024)(128)(4,1)S(1)} %broadcast_compare_fusion.4, ...), kind=kLoop, calls=%fused_computation.1 | loop fusion | flops 16220160 | bytes 43288960 | tf_op jit(solution)/shard_map/add | solution.py:66
  168.6 8.8 %copy.9 = f32[256,7040]{0,1:T(8,128)} copy(f32[256,7040]{1,0:T(8,128)} %fusion) | data formatting | bytes 14417920 | tf_op jit(solution)/shard_map/add | solution.py:66
  177.3 4.9 %reduce_sum.9 = f32[256,1408]{0,1:T(8,128)} reduce(f32[256,5,1408]{0,2,1:T(8,128)} %bitcast.30, f32[]{:T(128)} %constant.61.clone.1), dimensions={1}, to_apply=%region_0.1 | reduce | flops 1441792 | bytes 8650756 | tf_op jit(solution)/shard_map/reduce_sum | solution.py:67
  182.3 0.0 reduce-scatter.3.cloned.1.call-update
  182.3 0.6 dynamic-slice
  183.5 178.7 %all-reduce.3.cloned.1.call-done = f32[7040,384]{0,1:T(8,128)} async-done(((f32[7040,384]{0,1:T(8,128)}), f32[7040,384]{0,1:T(8,128)}) %all-reduce.3.cloned.1.call-update) | async-done | bytes 10813456
  362.3 1.1 constant_dynamic-slice_fusion
  363.4 0.8 copy.10
  364.2 1.7 convert_element_type.23
  (16 shorter events, 0.1 us)
Async XLA Ops:
  8.0 134.8 %copy-start = (bf16[256,1408]{1,0:T(8,128)(2,1)S(1)}, bf16[256,1408]{1,0:T(8,128)(2,1)}, u32[]{:S(2)}) copy-start(bf16[256,1408]{1,0:T(8,128)(2,1)} %param.4) | copy-start | bytes 2162692
  8.0 16.4 %copy-start.3 = (bf16[128,384]{1,0:T(8,128)(2,1)S(1)}, bf16[128,384]{1,0:T(8,128)(2,1)}, u32[]{:S(2)}) copy-start(bf16[128,384]{1,0:T(8,128)(2,1)} %param.6) | copy-start | bytes 294916
  11.9 12.9 %copy-start.2 = (bf16[256,384]{1,0:T(8,128)(2,1)S(1)}, bf16[256,384]{1,0:T(8,128)(2,1)}, u32[]{:S(2)}) copy-start(bf16[256,384]{1,0:T(8,128)(2,1)} %param.5) | copy-start | bytes 589828
  11.9 138.2 %all-to-all-start = ((bf16[64,110,384]{2,1,0:T(8,128)(2,1)}), bf16[64,110,384]{2,1,0:T(8,128)(2,1)}, u32[]{:S(2)}, u32[]{:S(2)}) async-start(bf16[64,110,384]{2,1,0:T(8,128)(2,1)} %stack.2), calls=%async_computation | async-start | bytes 11010048 | tf_op jit(solution)/shard_map/all_to_all | solution.py:59
  24.3 337.9 %all-reduce.3.cloned.1.call-start = ((), (), s32[]{:S(2)}) async-start(), calls=%async_computation.3 | async-start | bytes 21626880
  25.1 115.6 %collective-permute-start.1 = (bf16[2,384]{1,0:T(2,128)(2,1)S(1)}, bf16[2,384]{1,0:T(2,128)(2,1)S(1)}, u32[]{:S(2)}, u32[]{:S(2)}) collective-permute-start(bf16[2,384]{1,0:T(2,128)(2,1)S(1)} %get-tuple-element.9), channel_id=1, source_target_pairs={{4,0},{8,4},{12,8},{16,12},{20,16},{24,20},{28,24},{32,28},{36,32}... | collective-permute-start | bytes 4616 | tf_op jit(solution)/shard_map/ppermute | solution.py:19
  29.4 113.3 %collective-permute-start = (bf16[2,384]{1,0:T(2,128)(2,1)S(1)}, bf16[2,384]{1,0:T(2,128)(2,1)S(1)}, u32[]{:S(2)}, u32[]{:S(2)}) collective-permute-start(bf16[2,384]{1,0:T(2,128)(2,1)S(1)} %get-tuple-element.8), channel_id=1, source_target_pairs={{0,4},{4,8},{8,12},{12,16},{16,20},{20,24},{24,28},{28,32},{32,36}... | collective-permute-start | bytes 4616 | tf_op jit(solution)/shard_map/ppermute | solution.py:18
  150.0 214.3 %reduce-scatter.3.cloned.1.call-start = ((), (), s32[]{:S(2)}) async-start(), calls=%async_computation.2 | async-start | bytes 1802240 | tf_op jit(solution)/shard_map/reduce_scatter | solution.py:68
  168.6 197.3 %copy-start.1 = (bf16[256,1408]{1,0:T(8,128)(2,1)S(1)}, bf16[256,1408]{1,0:T(8,128)(2,1)}, u32[]{:S(2)}) copy-start(bf16[256,1408]{1,0:T(8,128)(2,1)} %param.4) | copy-start | bytes 2162692
  177.3 5.0 %copy-start.4 = (u32[256]{0:T(256)S(1)}, u32[256]{0:T(256)}, u32[]{:S(2)}) copy-start(u32[256]{0:T(256)} %constant.69) | copy-start | bytes 3076
Sparse Core Ops, SparseCore 0:
  150.1 212.1 all-reduce.2
Sparse Core Ops, SparseCore 1:
  182.4 29.2 reduce-scatter.2
